TPU v7x, 512 devices: a whole 4x8x8 slice. The times are simulated.
512 devices in a mesh: ctx: 64 (over y, z_hi, core), fsdp: 8 (over z_lo, x).
Axes of the slice: x: 4, y: 8, z: 8 (z_hi: 4, z_lo: 2; z = z_hi * 2 + z_lo), core: 2. Of those that a mesh axis runs over, the one named last changes fastest.
Arguments:
- query_act: bfloat16 [16384, 3072], P('ctx', 'fsdp'), may hold values from -10 to 10
- key_act: bfloat16 [16384, 3072], P('ctx', 'fsdp'), may hold values from -4 to 4
- value_act: bfloat16 [16384, 3072], P('ctx', 'fsdp'), may hold values from -6 to 6
- resid_in: bfloat16 [16384, 3072], P('ctx', 'fsdp'), may hold values from -60 to 60
- gate_vec: float32 [3072], P('fsdp'), may hold values from 0.5 to 2.5
- mod_scale: float32 [3072], P('fsdp'), may hold values from -2.5 to 2.5
- mod_shift: float32 [3072], P('fsdp'), may hold values from -3 to 3
- w_up: bfloat16 [3072, 6912], P(('ctx', 'fsdp')), may hold values from -0.109375 to 0.109375
- bias_up: float32 [6912], P('fsdp'), may hold values from -3 to 3
Outputs:
- residual: bfloat16 [16384, 3072], P('ctx', 'fsdp')
- hidden: bfloat16 [16384, 6912], P('ctx', 'fsdp')
All inputs are finite; a program needn't handle non-finite values.
Results may differ from a plain program's by a relative error of at most 0.0059.
Values may be sent and summed in bfloat16 or wider, within the bound.
A program may use at most 64 MiB of HBM per device.

v0:
```python
import math
import jax
import jax.numpy as jnp
from jax import lax
from jax.sharding import PartitionSpec as P

HEAD = 128
D = 3072


def padded_2(cells, sides, width):
    for axis, dim in sides:
        count = lax.axis_size(axis)
        ends = count - 1
        head = lax.slice_in_dim(cells, 0, width, axis=dim)
        tail = lax.slice_in_dim(cells, cells.shape[dim] - width, cells.shape[dim], axis=dim)
        cells = jnp.concatenate(
            [
                lax.ppermute(tail, axis, [(i, (i + 1) % count) for i in range(ends)]),
                cells,
                lax.ppermute(head, axis, [((i + 1) % count, i) for i in range(ends)]),
            ],
            axis=dim,
        )
    return cells


def shards(query_act, key_act, value_act, resid_in, gate_vec, mod_scale, mod_shift, w_up, bias_up):
    tok_rows = query_act.shape[0]
    feat_width = query_act.shape[1]
    reach_rows = tok_rows // 2
    ctx_count = lax.axis_size("ctx")
    seq_total = tok_rows * ctx_count
    stacked = jnp.stack([key_act, value_act])
    padded = padded_2(stacked, (("ctx", 1),), reach_rows)
    first_pos = lax.axis_index("ctx") * tok_rows
    query_pos = first_pos + jnp.arange(tok_rows, dtype=jnp.int32)
    key_pos = first_pos - reach_rows + jnp.arange(tok_rows + 2 * reach_rows, dtype=jnp.int32)
    allowed = (
        (jnp.abs(query_pos[:, None] - key_pos[None, :]) <= reach_rows)
        & (key_pos[None, :] >= 0)
        & (key_pos[None, :] < seq_total)
    )
    scale_qk = 1.0 / math.sqrt(HEAD)
    head_outputs = []
    for head_idx in range(feat_width // HEAD):
        head_cols = slice(head_idx * HEAD, (head_idx + 1) * HEAD)
        scores = (
            jnp.einsum(
                "qd,kd->qk",
                query_act[:, head_cols],
                padded[0, :, head_cols],
                preferred_element_type=jnp.float32,
            )
            * scale_qk
        )
        masked = jnp.where(allowed, scores, -jnp.inf)
        row_max = jnp.max(masked, axis=1, keepdims=True)
        exp_terms = jnp.exp(masked - row_max)
        attn_probs = (exp_terms / jnp.sum(exp_terms, axis=1, keepdims=True)).astype(jnp.bfloat16)
        head_outputs.append(
            jnp.dot(attn_probs, padded[1, :, head_cols], preferred_element_type=jnp.float32)
        )
    attended = jnp.concatenate(head_outputs, axis=1).astype(jnp.bfloat16)
    residual_out = (resid_in.astype(jnp.float32) + gate_vec * attended.astype(jnp.float32)).astype(
        jnp.bfloat16
    )
    rows_float = residual_out.astype(jnp.float32)
    row_sum = lax.psum(jnp.sum(rows_float, axis=1), "fsdp")
    mean_val = row_sum / D
    centered = rows_float - mean_val[:, None]
    var_val = lax.psum(jnp.sum(centered * centered, axis=1), "fsdp") / D
    normed = (
        centered * lax.rsqrt(var_val + 1e-06)[:, None] * (1.0 + mod_scale) + mod_shift
    ).astype(jnp.bfloat16)
    full_feat = lax.all_gather(normed, "fsdp", axis=1, tiled=True)
    strided = lax.all_gather(w_up, "ctx", axis=0, tiled=True)
    regrouped = lax.all_to_all(strided, "fsdp", split_axis=1, concat_axis=0, tiled=True)
    fsdp_count = lax.axis_size("fsdp")
    row_width = w_up.shape[0]
    permuted = (
        full_feat.reshape(tok_rows, ctx_count, fsdp_count, row_width)
        .transpose(0, 2, 1, 3)
        .reshape(tok_rows, -1)
    )
    pre_act = jnp.dot(permuted, regrouped, preferred_element_type=jnp.float32)
    hidden = jax.nn.gelu(pre_act + bias_up, approximate=True).astype(jnp.bfloat16)
    return (residual_out, hidden)


def solution(mesh):
    placed = (
        P("ctx", "fsdp"),
        P("ctx", "fsdp"),
        P("ctx", "fsdp"),
        P("ctx", "fsdp"),
        P("fsdp"),
        P("fsdp"),
        P("fsdp"),
        P(("ctx", "fsdp"), None),
        P("fsdp"),
    )
    return jax.shard_map(
        shards,
        mesh=mesh,
        in_specs=placed,
        out_specs=(P("ctx", "fsdp"), P("ctx", "fsdp")),
        check_vma=False,
    )
```

profile of v0, /device:TPU:8, one launch (start us, length us, event | category | flops | bytes accessed | tf_op | source)
XLA Modules:
  0.0 307.6 jit_solution(431408384966726718)
XLA Ops:
  8.0 0.0 all-gather.6.cloned.1.call-start
  8.0 0.7 all-gather.6.cloned.1.call-update
  8.7 106.1 %all-gather.6.cloned.1.call-done = bf16[64,6,6912]{2,1,0:T(8,128)(2,1)} async-done(((bf16[1,6,6912]{2,1,0:T(8,128)(2,1)}), bf16[64,6,6912]{2,1,0:T(8,128)(2,1)}) %all-gather.6.cloned.1.call-update) | async-done | bytes 5308432 | tf_op jit(solution)/shard_map/all_gather | solution.py:77
  114.8 13.9 %all_to_all.14 = bf16[384,8,864]{2,1,0:T(8,128)(2,1)} reshape(bf16[64,6,6912]{2,1,0:T(8,128)(2,1)} %all-gather.6.cloned.1.call-done) | data formatting | bytes 10616832 | tf_op jit(solution)/shard_map/all_to_all | solution.py:78
  128.7 8.4 %copy.19 = bf16[384,8,864]{0,2,1:T(8,128)(2,1)} copy(bf16[384,8,864]{2,1,0:T(8,128)(2,1)} %all_to_all.14) | data formatting | bytes 10616832 | tf_op jit(solution)/shard_map/all_to_all | solution.py:78
  137.2 0.0 copy-start
  137.2 0.0 copy-start.1
  137.2 0.0 copy-start.2
  137.2 0.0 copy-start.5
  137.2 4.8 %all-to-all-start = ((bf16[384,8,864]{0,2,1:T(8,128)(2,1)}), bf16[384,8,864]{0,2,1:T(8,128)(2,1)}, u32[]{:S(2)}, u32[]{:S(2)}) async-start(bf16[384,8,864]{0,2,1:T(8,128)(2,1)} %copy.19), calls=%async_computation | async-start | bytes 10616832 | tf_op jit(solution)/shard_map/all_to_all | solution.py:78
  142.0 0.0 copy-start.6
  142.0 0.0 all-gather.4.cloned.1.call-start
  142.1 0.0 copy-done
  142.1 0.0 copy-done.1
  142.1 2.2 collective-permute-start
  144.3 6.4 %collective-permute-start.1 = (bf16[2,128,384]{2,1,0:T(8,128)(2,1)S(1)}, bf16[2,128,384]{2,1,0:T(8,128)(2,1)S(1)}, u32[]{:S(2)}, u32[]{:S(2)}) collective-permute-start(bf16[2,128,384]{2,1,0:T(8,128)(2,1)S(1)} %get-tuple-element.11), channel_id=1, source_target_pairs={{8,0},{16,8},{24,16},{32,24},{40,32},{48,40},{56,48},{64,56},{72,6... | collective-permute-start | bytes 589832 | tf_op jit(solution)/shard_map/ppermute | solution.py:21
  150.8 0.0 copy-done.2
  150.8 0.1 copy.17
  151.0 0.0 copy-done.5
  151.0 3.2 %collective-permute-done = bf16[2,128,384]{2,1,0:T(8,128)(2,1)S(1)} collective-permute-done((bf16[2,128,384]{2,1,0:T(8,128)(2,1)S(1)}, bf16[2,128,384]{2,1,0:T(8,128)(2,1)S(1)}, u32[]{:S(2)}, u32[]{:S(2)}) %collective-permute-start) | collective-permute-done | bytes 196640 | tf_op jit(solution)/shard_map/ppermute | solution.py:19
  154.2 0.0 collective-permute-done.1
  154.2 0.1 pad_maximum_fusion
  154.2 0.0 copy-done.6
  154.3 0.3 fusion.31
  154.6 0.1 fusion.20
  154.7 0.3 fusion.32
  155.1 0.1 fusion.19
  155.2 0.3 fusion.33
  155.5 0.1 fusion.18
  155.7 0.3 convolution_convert_fusion
  155.9 0.3 convolution_convert_fusion.1
  156.2 0.0 copy-start.3
  156.2 0.0 copy-start.4
  156.2 0.3 convolution_convert_fusion.2
  156.5 0.4 copy-done.3
  156.9 0.2 convert_reduce_fusion
  157.0 60.3 %psum.14 = f32[256]{0:T(256)S(1)} all-reduce(f32[256]{0:T(256)S(1)} %get-tuple-element.8), channel_id=1, replica_groups=mesh['ctx'=64,'fsdp'=8] {'fsdp'}, use_global_device_ids=true, to_apply=%region_7.8 | all-reduce | flops 256 | bytes 2048 | tf_op jit(solution)/shard_map/psum | solution.py:69
  217.4 0.1 fusion.21
  217.5 18.2 %psum.15 = f32[256]{0:T(256)S(1)} all-reduce(f32[256]{0:T(256)S(1)} %fusion.21), channel_id=1, replica_groups=mesh['ctx'=64,'fsdp'=8] {'fsdp'}, use_global_device_ids=true, to_apply=%region_9.10 | all-reduce | flops 256 | bytes 2048 | tf_op jit(solution)/shard_map/psum | solution.py:72
  235.7 0.0 copy-done.4
  235.7 0.9 fusion.24
  236.5 0.0 all-gather.4.cloned.1.call-update
  236.6 0.8 copy.21
  237.4 50.2 %all-gather.4.cloned.1.call-done = bf16[256,3072]{0,1:T(8,128)(2,1)} async-done(((bf16[256,384]{0,1:T(8,128)(2,1)}), bf16[256,3072]{0,1:T(8,128)(2,1)}) %all-gather.4.cloned.1.call-update) | async-done | bytes 1572880 | tf_op jit(solution)/shard_map/all_gather | solution.py:76
  287.6 2.5 reshape.41
  290.1 1.5 copy.18
  291.6 2.6 reshape.42
  294.2 0.0 all-to-all-done
  294.2 0.0 copy-start.7
  294.2 3.5 %copy.22 = bf16[8,108,8,384]{3,2,0,1:T(8,128)(2,1)S(1)} copy(bf16[8,108,8,384]{3,2,1,0:T(8,128)(2,1)} %bitcast.14) | data formatting | bytes 10616832 | tf_op jit(solution)/shard_map/all_to_all | solution.py:78
  297.7 0.0 copy-done.7
  297.7 2.5 fusion.13
  (7 shorter events, 0.1 us)
Async XLA Ops:
  8.0 106.8 %all-gather.6.cloned.1.call-start = ((), (), s32[]{:S(2)}) async-start(), calls=%async_computation.2 | async-start | bytes 7188480 | tf_op jit(solution)/shard_map/all_gather | solution.py:77
  137.2 4.9 %copy-start = (bf16[256,384]{1,0:T(8,128)(2,1)S(1)}, bf16[256,384]{1,0:T(8,128)(2,1)}, u32[]{:S(2)}) copy-start(bf16[256,384]{1,0:T(8,128)(2,1)} %param.10) | copy-start | bytes 589828
  137.2 4.9 %copy-start.1 = (bf16[256,384]{1,0:T(8,128)(2,1)S(1)}, bf16[256,384]{1,0:T(8,128)(2,1)}, u32[]{:S(2)}) copy-start(bf16[256,384]{1,0:T(8,128)(2,1)} %param.11) | copy-start | bytes 589828
  137.2 13.6 %copy-start.2 = (bf16[256,384]{1,0:T(8,128)(2,1)S(1)}, bf16[256,384]{1,0:T(8,128)(2,1)}, u32[]{:S(2)}) copy-start(bf16[256,384]{1,0:T(8,128)(2,1)} %param.12) | copy-start | bytes 589828
  137.2 13.8 %copy-start.5 = (f32[384]{0:T(512)S(1)}, f32[384]{0:T(512)}, u32[]{:S(2)}) copy-start(f32[384]{0:T(512)} %param.14) | copy-start | bytes 4612
  137.2 157.0 %all-to-all-start = ((bf16[384,8,864]{0,2,1:T(8,128)(2,1)}), bf16[384,8,864]{0,2,1:T(8,128)(2,1)}, u32[]{:S(2)}, u32[]{:S(2)}) async-start(bf16[384,8,864]{0,2,1:T(8,128)(2,1)} %copy.19), calls=%async_computation | async-start | bytes 10616832 | tf_op jit(solution)/shard_map/all_to_all | solution.py:78
  142.0 12.2 %copy-start.6 = (bf16[256,384]{1,0:T(8,128)(2,1)S(1)}, bf16[256,384]{1,0:T(8,128)(2,1)}, u32[]{:S(2)}) copy-start(bf16[256,384]{1,0:T(8,128)(2,1)} %param.9) | copy-start | bytes 589828
  142.0 145.6 %all-gather.4.cloned.1.call-start = ((), (), s32[]{:S(2)}) async-start(), calls=%async_computation.1 | async-start | bytes 1769472 | tf_op jit(solution)/shard_map/all_gather | solution.py:76
  142.1 12.0 %collective-permute-start = (bf16[2,128,384]{2,1,0:T(8,128)(2,1)S(1)}, bf16[2,128,384]{2,1,0:T(8,128)(2,1)S(1)}, u32[]{:S(2)}, u32[]{:S(2)}) collective-permute-start(bf16[2,128,384]{2,1,0:T(8,128)(2,1)S(1)} %get-tuple-element.10), channel_id=1, source_target_pairs={{0,8},{8,16},{16,24},{24,32},{32,40},{40,48},{48,56},{56,64},{64,7... | collective-permute-start | bytes 589832 | tf_op jit(solution)/shard_map/ppermute | solution.py:19
  144.3 9.9 %collective-permute-start.1 = (bf16[2,128,384]{2,1,0:T(8,128)(2,1)S(1)}, bf16[2,128,384]{2,1,0:T(8,128)(2,1)S(1)}, u32[]{:S(2)}, u32[]{:S(2)}) collective-permute-start(bf16[2,128,384]{2,1,0:T(8,128)(2,1)S(1)} %get-tuple-element.11), channel_id=1, source_target_pairs={{8,0},{16,8},{24,16},{32,24},{40,32},{48,40},{56,48},{64,56},{72,6... | collective-permute-start | bytes 589832 | tf_op jit(solution)/shard_map/ppermute | solution.py:21
  156.2 0.7 copy-start.3
  156.2 79.5 %copy-start.4 = (f32[384]{0:T(512)S(1)}, f32[384]{0:T(512)}, u32[]{:S(2)}) copy-start(f32[384]{0:T(512)} %param.15) | copy-start | bytes 4612
  294.2 3.5 %copy-start.7 = (f32[864]{0:T(1024)S(1)}, f32[864]{0:T(1024)}, u32[]{:S(2)}) copy-start(f32[864]{0:T(1024)} %param.17) | copy-start | bytes 10372
Sparse Core Ops, SparseCore 0:
  12.1 102.6 all-gather.5
Sparse Core Ops, SparseCore 1:
  236.7 50.9 all-gather.3
where the time goes:
time: 308 us
  waiting for transfers between devices  160 us (52%)
  blocking collectives  78.5 us (25%)
  local copies, waits for them, and re-layouts  33.8 us (11%)
  between operations  15.7 us (5%)
  starting transfers between devices  13.5 us (4%)
  matrix products  4.25 us (1%)
    all_gather x1, waiting for transfers between devices, shards(): strided = lax.all_gather(w_up, 'ctx', axis=0, tiled=True)  106 us
    psum x1, blocking collectives, shards(): row_sum = lax.psum(jnp.sum(rows_float, axis=1), 'fsdp')  60.3 us
    all_gather x1, waiting for transfers between devices, shards(): full_feat = lax.all_gather(normed, 'fsdp', axis=1, tiled=True)  50.2 us
    all_to_all x3, local copies, waits for them, and re-layouts, shards(): lax.all_to_all(strided, 'fsdp', split_axis=1, concat_axis=0, tiled=True)  25.9 us
    psum x1, blocking collectives, shards(): var_val = lax.psum(jnp.sum(centered * centered, axis=1), 'fsdp') / D  18.2 us
    ppermute x1, starting transfers between devices, padded_2(): lax.ppermute(head, axis, [((i + 1) % count, i) for i in range(ends)])  6.43 us
  transfers between devices with their start and end apart: 5, of which 3 were waited for; matrix products, arithmetic and copies ran while one was open for 4% of the time, Pallas kernels for 0%

commit v1 on v0

--- a/solution.py
+++ b/solution.py
@@ -74,7 +74,10 @@
         centered * lax.rsqrt(var_val + 1e-06)[:, None] * (1.0 + mod_scale) + mod_shift
     ).astype(jnp.bfloat16)
     full_feat = lax.all_gather(normed, "fsdp", axis=1, tiled=True)
-    strided = lax.all_gather(w_up, "ctx", axis=0, tiled=True)
+    tails_group = lambda t0, row_axis: jnp.concatenate(
+        lax.all_to_all(jnp.stack([t0] * lax.axis_size(row_axis), 0), row_axis, 0, 0), 0
+    )
+    strided = tails_group(w_up, "ctx")
     regrouped = lax.all_to_all(strided, "fsdp", split_axis=1, concat_axis=0, tiled=True)
     fsdp_count = lax.axis_size("fsdp")
     row_width = w_up.shape[0]

time: 308 us -> 393 us (1.28)
  blocking collectives: 78.5 us -> 259 us
  waiting for transfers between devices: 160 us -> 68.8 us
  starting transfers between devices: 13.5 us -> 9.21 us
    all_to_all x0 -> x1, blocking collectives: none -> 182 us  [shards(): lax.all_to_all(jnp.stack([t0] * lax.axis_size(row_axis), 0), row_axis, 0, 0)]
    all_gather x1 -> x0, waiting for transfers between devices: 106 us -> none  [shards(): strided = lax.all_gather(w_up, 'ctx', axis=0, tiled=True)]
    all_gather x1, waiting for transfers between devices: 50.2 us -> 59.9 us  [shards(): full_feat = lax.all_gather(normed, 'fsdp', axis=1, tiled=True)]
    ppermute x1, waiting for transfers between devices: 3.18 us -> 8.41 us  [padded_2(): lax.ppermute(tail, axis, [(i, (i + 1) % count) for i in range(ends)])]
    ppermute x1, starting transfers between devices: 6.43 us -> 1.92 us  [padded_2(): lax.ppermute(head, axis, [((i + 1) % count, i) for i in range(ends)])]
  transfers between devices with their start and end apart: 5 -> 4, of which waited for: 3 -> 3; matrix products, arithmetic and copies ran while one was open for 4% -> 3% of each run, Pallas kernels for 0% -> 0%
where the time goes in v1:
time: 393 us; the launch traced here: 392 us
  blocking collectives  259 us (66%)
  waiting for transfers between devices  68.8 us (18%)
  local copies, waits for them, and re-layouts  35.2 us (9%)
  between operations  14.3 us (4%)
  starting transfers between devices  9.21 us (2%)
  matrix products  4.25 us (1%)
    all_to_all x1, blocking collectives, shards(): lax.all_to_all(jnp.stack([t0] * lax.axis_size(row_axis), 0), row_axis, 0, 0)  182 us
    all_gather x1, waiting for transfers between devices, shards(): full_feat = lax.all_gather(normed, 'fsdp', axis=1, tiled=True)  59.9 us
    psum x1, blocking collectives, shards(): row_sum = lax.psum(jnp.sum(rows_float, axis=1), 'fsdp')  58.7 us
    all_to_all x3, local copies, waits for them, and re-layouts, shards(): lax.all_to_all(strided, 'fsdp', split_axis=1, concat_axis=0, tiled=True)  25.9 us
    psum x1, blocking collectives, shards(): var_val = lax.psum(jnp.sum(centered * centered, axis=1), 'fsdp') / D  18.2 us
    ppermute x1, waiting for transfers between devices, padded_2(): lax.ppermute(tail, axis, [(i, (i + 1) % count) for i in range(ends)])  8.41 us
  transfers between devices with their start and end apart: 4, of which 3 were waited for; matrix products, arithmetic and copies ran while one was open for 3% of the time, Pallas kernels for 0%

profile of v1, /device:TPU:8, one launch (start us, length us, event | category | flops | bytes accessed | tf_op | source)
XLA Modules:
  0.0 392.0 jit_solution(4904293495325251307)
XLA Ops:
  7.2 1.4 stack.11
  8.5 181.8 %all_to_all.24 = bf16[64,6,6912]{2,1,0:T(8,128)(2,1)} all-to-all(bf16[64,6,6912]{2,1,0:T(8,128)(2,1)S(1)} %stack.11), channel_id=1, replica_groups=mesh['ctx'=64,'fsdp'=8] {'ctx'}, dimensions={0} | all-to-all | bytes 10616832 | tf_op jit(solution)/shard_map/all_to_all | solution.py:78
  190.3 13.9 %all_to_all.18 = bf16[384,8,864]{2,1,0:T(8,128)(2,1)} reshape(bf16[64,6,6912]{2,1,0:T(8,128)(2,1)} %all_to_all.24) | data formatting | bytes 10616832 | tf_op jit(solution)/shard_map/all_to_all | solution.py:81
  204.2 8.4 %copy.19 = bf16[384,8,864]{0,2,1:T(8,128)(2,1)} copy(bf16[384,8,864]{2,1,0:T(8,128)(2,1)} %all_to_all.18) | data formatting | bytes 10616832 | tf_op jit(solution)/shard_map/all_to_all | solution.py:81
  212.7 0.0 copy-start
  212.7 0.0 copy-start.1
  212.7 0.0 copy-start.2
  212.7 0.0 copy-start.5
  212.7 4.8 %all-to-all-start.1 = ((bf16[384,8,864]{0,2,1:T(8,128)(2,1)}), bf16[384,8,864]{0,2,1:T(8,128)(2,1)}, u32[]{:S(2)}, u32[]{:S(2)}) async-start(bf16[384,8,864]{0,2,1:T(8,128)(2,1)} %copy.19), calls=%async_computation.1 | async-start | bytes 10616832 | tf_op jit(solution)/shard_map/all_to_all | solution.py:81
  217.5 0.0 copy-start.6
  217.6 0.0 all-gather.2.cloned.1.call-start
  217.6 0.0 copy-done
  217.6 0.0 copy-done.1
  217.7 1.9 collective-permute-start.1
  219.6 2.4 collective-permute-start
  222.0 0.0 copy-done.2
  222.0 0.1 copy.17
  222.2 0.0 copy-done.5
  222.3 0.5 collective-permute-done.1
  222.8 8.4 %collective-permute-done = bf16[2,128,384]{2,1,0:T(8,128)(2,1)S(1)} collective-permute-done((bf16[2,128,384]{2,1,0:T(8,128)(2,1)S(1)}, bf16[2,128,384]{2,1,0:T(8,128)(2,1)S(1)}, u32[]{:S(2)}, u32[]{:S(2)}) %collective-permute-start) | collective-permute-done | bytes 196640 | tf_op jit(solution)/shard_map/ppermute | solution.py:19
  231.2 0.1 pad_maximum_fusion
  231.3 0.0 copy-done.6
  231.3 0.3 fusion.31
  231.6 0.1 fusion.20
  231.7 0.3 fusion.32
  232.1 0.1 fusion.19
  232.2 0.3 fusion.33
  232.6 0.1 fusion.18
  232.7 0.3 convolution_convert_fusion
  232.9 0.3 convolution_convert_fusion.1
  233.2 0.0 copy-start.3
  233.2 0.0 copy-start.4
  233.2 0.3 convolution_convert_fusion.2
  233.5 0.4 copy-done.3
  233.9 0.2 convert_reduce_fusion
  234.0 58.7 %psum.14 = f32[256]{0:T(256)S(1)} all-reduce(f32[256]{0:T(256)S(1)} %get-tuple-element.8), channel_id=1, replica_groups=mesh['ctx'=64,'fsdp'=8] {'fsdp'}, use_global_device_ids=true, to_apply=%region_7.8 | all-reduce | flops 256 | bytes 2048 | tf_op jit(solution)/shard_map/psum | solution.py:69
  292.7 0.1 fusion.21
  292.8 18.2 %psum.15 = f32[256]{0:T(256)S(1)} all-reduce(f32[256]{0:T(256)S(1)} %fusion.21), channel_id=1, replica_groups=mesh['ctx'=64,'fsdp'=8] {'fsdp'}, use_global_device_ids=true, to_apply=%region_9.10 | all-reduce | flops 256 | bytes 2048 | tf_op jit(solution)/shard_map/psum | solution.py:72
  311.0 0.0 copy-done.4
  311.0 0.9 fusion.24
  311.9 0.0 all-gather.2.cloned.1.call-update
  311.9 0.8 copy.21
  312.7 59.9 %all-gather.2.cloned.1.call-done = bf16[256,3072]{0,1:T(8,128)(2,1)} async-done(((bf16[256,384]{0,1:T(8,128)(2,1)}), bf16[256,3072]{0,1:T(8,128)(2,1)}) %all-gather.2.cloned.1.call-update) | async-done | bytes 1572880 | tf_op jit(solution)/shard_map/all_gather | solution.py:76
  372.6 2.5 reshape.45
  375.1 1.5 copy.18
  376.6 2.6 reshape.46
  379.1 0.0 all-to-all-done.1
  379.2 0.0 copy-start.7
  379.2 3.5 copy.22
  382.7 0.0 copy-done.7
  382.7 2.5 fusion.13
  (7 shorter events, 0.1 us)
Async XLA Ops:
  212.7 4.9 %copy-start = (bf16[256,384]{1,0:T(8,128)(2,1)S(1)}, bf16[256,384]{1,0:T(8,128)(2,1)}, u32[]{:S(2)}) copy-start(bf16[256,384]{1,0:T(8,128)(2,1)} %param.10) | copy-start | bytes 589828
  212.7 4.9 %copy-start.1 = (bf16[256,384]{1,0:T(8,128)(2,1)S(1)}, bf16[256,384]{1,0:T(8,128)(2,1)}, u32[]{:S(2)}) copy-start(bf16[256,384]{1,0:T(8,128)(2,1)} %param.11) | copy-start | bytes 589828
  212.7 9.3 %copy-start.2 = (bf16[256,384]{1,0:T(8,128)(2,1)S(1)}, bf16[256,384]{1,0:T(8,128)(2,1)}, u32[]{:S(2)}) copy-start(bf16[256,384]{1,0:T(8,128)(2,1)} %param.12) | copy-start | bytes 589828
  212.7 9.5 %copy-start.5 = (f32[384]{0:T(512)S(1)}, f32[384]{0:T(512)}, u32[]{:S(2)}) copy-start(f32[384]{0:T(512)} %param.14) | copy-start | bytes 4612
  212.7 166.4 %all-to-all-start.1 = ((bf16[384,8,864]{0,2,1:T(8,128)(2,1)}), bf16[384,8,864]{0,2,1:T(8,128)(2,1)}, u32[]{:S(2)}, u32[]{:S(2)}) async-start(bf16[384,8,864]{0,2,1:T(8,128)(2,1)} %copy.19), calls=%async_computation.1 | async-start | bytes 10616832 | tf_op jit(solution)/shard_map/all_to_all | solution.py:81
  217.5 13.7 %copy-start.6 = (bf16[256,384]{1,0:T(8,128)(2,1)S(1)}, bf16[256,384]{1,0:T(8,128)(2,1)}, u32[]{:S(2)}) copy-start(bf16[256,384]{1,0:T(8,128)(2,1)} %param.9) | copy-start | bytes 589828
  217.6 155.1 %all-gather.2.cloned.1.call-start = ((), (), s32[]{:S(2)}) async-start(), calls=%async_computation.2 | async-start | bytes 1769472 | tf_op jit(solution)/shard_map/all_gather | solution.py:76
  217.7 5.1 %collective-permute-start.1 = (bf16[2,128,384]{2,1,0:T(8,128)(2,1)S(1)}, bf16[2,128,384]{2,1,0:T(8,128)(2,1)S(1)}, u32[]{:S(2)}, u32[]{:S(2)}) collective-permute-start(bf16[2,128,384]{2,1,0:T(8,128)(2,1)S(1)} %get-tuple-element.11), channel_id=1, source_target_pairs={{8,0},{16,8},{24,16},{32,24},{40,32},{48,40},{56,48},{64,56},{72,6... | collective-permute-start | bytes 589832 | tf_op jit(solution)/shard_map/ppermute | solution.py:21
  219.6 11.6 %collective-permute-start = (bf16[2,128,384]{2,1,0:T(8,128)(2,1)S(1)}, bf16[2,128,384]{2,1,0:T(8,128)(2,1)S(1)}, u32[]{:S(2)}, u32[]{:S(2)}) collective-permute-start(bf16[2,128,384]{2,1,0:T(8,128)(2,1)S(1)} %get-tuple-element.10), channel_id=1, source_target_pairs={{0,8},{8,16},{16,24},{24,32},{32,40},{40,48},{48,56},{56,64},{64,7... | collective-permute-start | bytes 589832 | tf_op jit(solution)/shard_map/ppermute | solution.py:19
  233.2 0.7 copy-start.3
  233.2 77.8 %copy-start.4 = (f32[384]{0:T(512)S(1)}, f32[384]{0:T(512)}, u32[]{:S(2)}) copy-start(f32[384]{0:T(512)} %param.15) | copy-start | bytes 4612
  379.2 3.5 copy-start.7
Sparse Core Ops, SparseCore 0:
  312.0 60.5 all-gather.1
